TPU v7x, 32 devices: a whole 2x2x4 slice. The times are simulated.
32 devices in a mesh: row: 2 (over x), col: 8 (over z, core), freq: 2 (over y).
Axes of the slice: x: 2, y: 2, z: 4, core: 2. Of those that a mesh axis runs over, the one named last changes fastest.
Arguments:
- left_data: float32 [2, 2048, 512], P(None, ('freq', 'row'), 'col'), parts along dimension 1, may hold values from -6 to 6
- right_data: float32 [2, 512, 8192], P(None, 'row', ('freq', 'col')), parts along dimension 2, may hold values from -0.1875 to 0.1875
Outputs:
- multiples: float32 [2, 2048, 4096], P(None, ('freq', 'row'), 'col'), parts along dimension 1
There are 2 independent parts, one for each index of `freq`. A program takes and returns all parts, laid end to end along the dimension named above; each array names one. Nothing has to cross between parts.
All inputs are finite; a program needn't handle non-finite values.
Results may differ from a plain program's by a relative error of at most 0.000071.
Values sent between devices are 32-bit elements; how exact they have to be, the bound alone decides.
A program may use at most 64 MiB of HBM per device.

v0:
```python
import jax
import jax.numpy as jnp
from jax import lax
from jax.sharding import PartitionSpec as P


def matmul_hi(a, b):
    return jnp.dot(a, b, preferred_element_type=jnp.float32, precision=lax.Precision.HIGHEST)


def complex_term(left_piece, right_piece):
    first = matmul_hi(left_piece[0], right_piece[0])
    second = matmul_hi(left_piece[1], right_piece[1])
    third = matmul_hi(left_piece[0] + left_piece[1], right_piece[0] + right_piece[1])
    return jnp.stack([first - second, third - first - second], axis=0)


def body(left_data, right_data):
    right_whole = lax.all_gather(right_data, "row", axis=1, tiled=True)
    left_full = lax.all_gather(left_data, "col", axis=2, tiled=True)
    return complex_term(left_full, right_whole)


def solution(mesh):
    placed = (P(None, ("freq", "row"), "col"), P(None, "row", ("freq", "col")))
    return jax.shard_map(
        body, mesh=mesh, in_specs=placed, out_specs=P(None, ("freq", "row"), "col"), check_vma=False
    )
```

profile of v0, /device:TPU:0, one launch (start us, length us, event | category | flops | bytes accessed | tf_op | source)
XLA Modules:
  0.0 93.9 jit_solution(1876528100538173473)
XLA Ops:
  6.5 0.0 all-gather.5.cloned.1.call-start
  6.5 0.7 all-gather.5.cloned.1.call-update
  7.3 0.0 all-gather.3.cloned.1.call-start
  7.3 0.7 all-gather.3.cloned.1.call-update
  8.0 36.7 %all-gather.5.cloned.1.call-done = f32[2,512,512]{2,1,0:T(8,128)} async-done(((f32[2,256,512]{2,1,0:T(8,128)}), f32[2,512,512]{2,1,0:T(8,128)}) %all-gather.5.cloned.1.call-update) | async-done | bytes 2097168 | tf_op jit(solution)/shard_map/all_gather | solution.py:19
  44.7 0.0 copy-start
  44.7 30.8 %all-gather.3.cloned.1.call-done = f32[2,512,512]{1,2,0:T(8,128)} async-done(((f32[2,512,64]{1,2,0:T(8,128)}), f32[2,512,512]{1,2,0:T(8,128)}) %all-gather.3.cloned.1.call-update) | async-done | bytes 2097168 | tf_op jit(solution)/shard_map/all_gather | solution.py:20
  75.5 3.4 %fusion.4 = f32[512,512]{1,0:T(8,128)S(1)} fusion(f32[2,512,512]{2,1,0:T(8,128)} %all-gather.5.cloned.1.call-done, f32[2,512,512]{1,2,0:T(8,128)} %all-gather.3.cloned.1.call-done), kind=kOutput, calls=%fused_computation.6 | convolution fusion | flops 1610612736 | bytes 3145728 | tf_op jit(solution)/shard_map/dot_general | solution.py:8
  78.9 0.0 copy-done
  78.9 3.1 %fusion.7 = f32[512,512]{1,0:T(8,128)S(1)} fusion(f32[2,512,512]{2,1,0:T(8,128)S(1)} %copy-done, f32[2,512,512]{1,2,0:T(8,128)} %all-gather.3.cloned.1.call-done), kind=kOutput, calls=%fused_computation.9 | convolution fusion | flops 1610612736 | bytes 3145728 | tf_op jit(solution)/shard_map/dot_general | solution.py:8
  82.0 0.0 copy-start.1
  82.0 0.2 subtract_bitcast_fusion
  82.2 1.4 %copy-done.1 = f32[2,512,512]{1,2,0:T(8,128)S(1)} copy-done((f32[2,512,512]{1,2,0:T(8,128)S(1)}, f32[2,512,512]{1,2,0:T(8,128)}, u32[]{:S(2)}) %copy-start.1) | copy-done | bytes 2097176
  83.6 2.0 %fusion.1 = f32[1,512,512]{2,1,0:T(8,128)S(1)} fusion(f32[512,512]{1,0:T(8,128)S(1)} %fusion.4, f32[512,512]{1,0:T(8,128)S(1)} %fusion.7, f32[2,512,512]{2,1,0:T(8,128)S(1)} %copy-done, f32[2,512,512]{1,2,0:T(8,128)S(1)} %copy-done.1), kind=kOutput, calls=%fused_computation.3 | convolution fusion | flops 1611661312 | bytes 7340032 | tf_op jit(solution)/shard_map/dot_general | solution.py:8
  85.6 1.5 %pad_maximum_fusion = f32[2,512,512]{2,1,0:T(8,128)} fusion(f32[1,512,512]{2,1,0:T(8,128)S(1)} %fusion.1, f32[1,512,512]{2,1,0:T(8,128)S(1)} %subtract_bitcast_fusion), kind=kLoop, calls=%fused_computation | loop fusion | flops 524288 | bytes 4194304 | tf_op jit(solution)/shard_map/stack | solution.py:15
Async XLA Ops:
  6.5 38.2 %all-gather.5.cloned.1.call-start = ((), (), s32[]{:S(2)}) async-start(), calls=%async_computation.1 | async-start | bytes 3145728 | tf_op jit(solution)/shard_map/all_gather | solution.py:19
  7.3 68.3 %all-gather.3.cloned.1.call-start = ((), (), s32[]{:S(2)}) async-start(), calls=%async_computation | async-start | bytes 2359296 | tf_op jit(solution)/shard_map/all_gather | solution.py:20
  44.7 34.2 %copy-start = (f32[2,512,512]{2,1,0:T(8,128)S(1)}, f32[2,512,512]{2,1,0:T(8,128)}, u32[]{:S(2)}) copy-start(f32[2,512,512]{2,1,0:T(8,128)} %all-gather.5.cloned.1.call-done) | copy-start | bytes 6291460
  82.0 1.6 %copy-start.1 = (f32[2,512,512]{1,2,0:T(8,128)S(1)}, f32[2,512,512]{1,2,0:T(8,128)}, u32[]{:S(2)}) copy-start(f32[2,512,512]{1,2,0:T(8,128)} %all-gather.3.cloned.1.call-done) | copy-start | bytes 6291460
Sparse Core Ops, SparseCore 0:
  8.9 35.8 all-gather.4
  46.3 29.1 all-gather.2
where the time goes:
time: 94.1 us; the launch traced here: 93.9 us
  waiting for transfers between devices  68.9 us (73%)
  between operations  13.4 us (14%)
  matrix products  8.41 us (9%)
  other arithmetic  1.7 us (2%)
  local copies, waits for them, and re-layouts  1.37 us (1%)
    all_gather x1, waiting for transfers between devices, body(): right_whole = lax.all_gather(right_data, 'row', axis=1, tiled=True)  36.7 us
    all_gather x1, waiting for transfers between devices, body(): left_full = lax.all_gather(left_data, 'col', axis=2, tiled=True)  30.8 us
    dot_general x3, matrix products, matmul_hi(): jnp.dot(a, b, preferred_element_type=jnp.float32, precision=lax.Precision...  8.41 us
  transfers between devices with their start and end apart: 2, of which 2 were waited for; matrix products, arithmetic and copies ran while one was open for 0% of the time, Pallas kernels for 0%

commit v1 on v0

v1 whole, which is shorter than its diff:
```python
import functools

import jax
import jax.numpy as jnp
from jax import lax
from jax.experimental import pallas as pl
from jax.experimental.pallas import tpu as pltpu
from jax.sharding import PartitionSpec as P

MESH = pl.DeviceIdType.MESH
LANES = 128


def split(value):
    high = value.astype(jnp.bfloat16)
    return high, (value - high.astype(jnp.float32)).astype(jnp.bfloat16)


def dot(a, b):
    return jnp.dot(a, b, preferred_element_type=jnp.float32)


def kernel(
    n_row, n_col, left_hbm, right_hbm, out_ref,
    left_f32, right_f32, left_hi, left_lo, w_hi, w_lo,
    own_sem, left_send, left_recv, right_send, right_recv,
):
    _, kb, rows = left_hbm.shape
    _, kr, cols = right_hbm.shape
    depth = kb * n_col
    chunks = cols // LANES
    line = n_col // 2

    x = lax.axis_index("row")
    place = lax.axis_index("col")
    z, core = place // 2, lax.rem(place, 2)
    has_next, has_prev = z + 1 < line, z >= 1

    def at(zz, cc):
        return {"col": zz * 2 + cc}

    def peer(d):
        return lax.rem(x + d, n_row)

    barrier = pltpu.get_barrier_semaphore()
    for d in range(1, n_row):
        pl.semaphore_signal(barrier, inc=1, device_id={"row": peer(d)}, device_id_type=MESH)

    @pl.when(has_next)
    def _():
        pl.semaphore_signal(barrier, inc=1, device_id=at(z + 1, core), device_id_type=MESH)

    @pl.when(has_prev)
    def _():
        pl.semaphore_signal(barrier, inc=1, device_id=at(z - 1, core), device_id_type=MESH)

    pl.semaphore_signal(barrier, inc=1, device_id=at(z, 1 - core), device_id_type=MESH)

    own_right = pltpu.make_async_copy(
        right_hbm, right_f32.at[:, pl.ds(pl.multiple_of(x * kr, 8), kr), :], own_sem.at[0])
    own_right.start()
    own_left = pltpu.make_async_copy(
        left_hbm, left_f32.at[:, pl.ds(pl.multiple_of(place * kb, 8), kb), :], own_sem.at[1])
    own_left.start()

    pl.semaphore_wait(barrier, n_row + has_next.astype(jnp.int32) + has_prev.astype(jnp.int32))

    def right_copy(d, j):
        return pltpu.make_async_remote_copy(
            src_ref=right_hbm.at[:, :, pl.ds(j * LANES, LANES)],
            dst_ref=right_f32.at[:, pl.ds(pl.multiple_of(x * kr, 8), kr), pl.ds(j * LANES, LANES)],
            send_sem=right_send.at[d - 1, j],
            recv_sem=right_recv.at[d - 1, j],
            device_id={"row": peer(d)},
            device_id_type=MESH,
        )

    def left_slot(zz, cc, part):
        return left_f32.at[part, pl.ds(pl.multiple_of((zz * 2 + cc) * kb, 8), kb), :]

    def left_copy(way, zz, cc, part, target, own=False):
        return pltpu.make_async_remote_copy(
            src_ref=left_hbm.at[part] if own else left_slot(zz, cc, part),
            dst_ref=left_slot(zz, cc, part),
            send_sem=left_send.at[way, zz, part],
            recv_sem=left_recv.at[cc, zz, part],
            device_id=target,
            device_id_type=MESH,
        )

    def up(zz, part, own=False):
        return left_copy(0, zz, core, part, at(z + 1, core), own)

    def down(zz, part, own=False):
        return left_copy(1, zz, core, part, at(z - 1, core), own)

    def across(zz, part, own=False):
        return left_copy(2, zz, core, part, at(z, 1 - core), own)

    def arrived(zz, cc, part):
        left_copy(2, zz, cc, part, at(z, 1 - core)).wait_recv()

    for part in range(2):
        @pl.when(has_next)
        def _():
            up(z, part, True).start()

        @pl.when(has_prev)
        def _():
            down(z, part, True).start()

    for j in range(chunks):
        for d in range(1, n_row):
            right_copy(d, j).start()
    for part in range(2):
        across(z, part, True).start()

    def to_weights(source_row, j, n):
        span = pl.ds(pl.multiple_of(source_row, 8), n)
        re = split(right_f32[0, span, j * LANES:(j + 1) * LANES])
        im = split(right_f32[1, span, j * LANES:(j + 1) * LANES])
        below = pl.ds(pl.multiple_of(depth + source_row, 8), n)
        for w, a, b in ((w_hi, re[0], im[0]), (w_lo, re[1], im[1])):
            w[j, span, :LANES] = a
            w[j, span, LANES:] = b
            w[j, below, :LANES] = -b
            w[j, below, LANES:] = a

    def convert(g):
        for part in range(2):
            block = left_f32[part, pl.ds(pl.multiple_of(g * LANES, LANES), LANES), :].T
            high, low = split(block)
            where = pl.ds(pl.multiple_of(part * depth + g * LANES, LANES), LANES)
            left_hi[:, where] = high
            left_lo[:, where] = low

    def partner_arrived(zz):
        for part in range(2):
            arrived(zz, 1 - core, part)

    def settle(zz):
        partner_arrived(zz)
        if 2 * kb == LANES:
            convert(zz)

    def right_arrived(j):
        for d in range(1, n_row):
            right_copy(d, j).wait_recv()
            to_weights(lax.rem(x + n_row - d, n_row) * kr, j, kr)

    own_right.wait()
    for j in range(chunks):
        to_weights(x * kr, j, kr)
    own_left.wait()

    for d in range(1, line):
        for part in range(2):
            @pl.when(z - d >= 0)
            def _():
                arrived(z - d, core, part)

                @pl.when(has_next)
                def _():
                    up(z - d, part).start()

                across(z - d, part).start()

            @pl.when(z + d < line)
            def _():
                arrived(z + d, core, part)

                @pl.when(has_prev)
                def _():
                    down(z + d, part).start()

                across(z + d, part).start()

        if d == 1:
            settle(z)
        else:
            @pl.when(z - (d - 1) >= 0)
            def _():
                settle(z - (d - 1))

            @pl.when(z + (d - 1) < line)
            def _():
                settle(z + (d - 1))

        if d - 1 < chunks - 1:
            right_arrived(d - 1)

    if line == 1:
        settle(z)
    else:
        @pl.when(z - (line - 1) >= 0)
        def _():
            settle(z - (line - 1))

        @pl.when(z + (line - 1) < line)
        def _():
            settle(z + (line - 1))

    if 2 * kb != LANES:
        for g in range(depth // LANES):
            convert(g)

    for j in range(chunks):
        if j >= min(line - 1, chunks - 1):
            right_arrived(j)
        total = dot(left_hi[...], w_hi[j]) + (dot(left_hi[...], w_lo[j]) + dot(left_lo[...], w_hi[j]))
        out_ref[0, :, j * LANES:(j + 1) * LANES] = total[:, :LANES]
        out_ref[1, :, j * LANES:(j + 1) * LANES] = total[:, LANES:]

    for j in range(chunks):
        for d in range(1, n_row):
            right_copy(d, j).wait_send()
    for part in range(2):
        for d in range(line):
            own = d == 0

            @pl.when(z - d >= 0)
            def _():
                @pl.when(has_next)
                def _():
                    up(z - d, part, own).wait_send()

                across(z - d, part, own).wait_send()

            @pl.when(z + d < line)
            def _():
                @pl.when(has_prev)
                def _():
                    down(z + d, part, own).wait_send()

                if d > 0:
                    across(z + d, part).wait_send()


def body(n_row, n_col, left_data, right_data):
    left = jnp.swapaxes(left_data, 1, 2)
    _, kb, rows = left.shape
    _, kr, cols = right_data.shape
    depth, chunks, line = kb * n_col, cols // LANES, n_col // 2
    return pl.pallas_call(
        functools.partial(kernel, n_row, n_col),
        out_shape=jax.ShapeDtypeStruct((2, rows, cols), jnp.float32),
        in_specs=[pl.BlockSpec(memory_space=pl.ANY)] * 2,
        out_specs=pl.BlockSpec(memory_space=pltpu.VMEM),
        scratch_shapes=[
            pltpu.VMEM((2, depth, rows), jnp.float32),
            pltpu.VMEM((2, depth, cols), jnp.float32),
            pltpu.VMEM((rows, 2 * depth), jnp.bfloat16),
            pltpu.VMEM((rows, 2 * depth), jnp.bfloat16),
            pltpu.VMEM((chunks, 2 * depth, 2 * LANES), jnp.bfloat16),
            pltpu.VMEM((chunks, 2 * depth, 2 * LANES), jnp.bfloat16),
            pltpu.SemaphoreType.DMA((2,)),
            pltpu.SemaphoreType.DMA((3, line, 2)),
            pltpu.SemaphoreType.DMA((2, line, 2)),
            pltpu.SemaphoreType.DMA((n_row - 1, chunks)),
            pltpu.SemaphoreType.DMA((n_row - 1, chunks)),
        ],
        compiler_params=pltpu.CompilerParams(
            collective_id=0, has_side_effects=True, vmem_limit_bytes=48 * 1024 * 1024),
    )(left, right_data)


def solution(mesh):
    placed = (P(None, ("freq", "row"), "col"), P(None, "row", ("freq", "col")))
    return jax.shard_map(
        functools.partial(body, mesh.shape["row"], mesh.shape["col"]),
        mesh=mesh, in_specs=placed, out_specs=P(None, ("freq", "row"), "col"), check_vma=False,
    )
```

time: 94.1 us -> 33.4 us (0.35)
  waiting for transfers between devices: 68.9 us -> 0 us
  Pallas kernels: 0 us -> 29.7 us
  between operations: 13.4 us -> 0.01 us
  matrix products: 8.41 us -> 0 us
  local copies, waits for them, and re-layouts: 1.37 us -> 3.5 us
  other arithmetic: 1.7 us -> 0 us
    all_gather x2 -> x0, waiting for transfers between devices: 67.5 us -> none  [the longest x1 36.7 us: body(): right_whole = lax.all_gather(right_data, 'row', axis=1, tiled=True)]
    pallas_call x0 -> x1, Pallas kernels: none -> 29.7 us  [body(): pl.pallas_call(functools.partial(kernel, n_row, n_col), out_shape=jax.Sha...]
    dot_general x3 -> x0, matrix products: 8.41 us -> none  [matmul_hi(): jnp.dot(a, b, preferred_element_type=jnp.float32, precision=lax.Precision...]
    unnamed x4 -> x5, local copies, waits for them, and re-layouts: 1.37 us -> 3.5 us
    another operation x2 -> x0, other arithmetic: 1.7 us -> none  [complex_term(): return jnp.stack([first - second, third - first - second], axis=0)]
    unnamed x2 -> x0, waiting for transfers between devices: 1.41 us -> none
  transfers between devices with their start and end apart: 2 -> 0, of which waited for: 2 -> 0; matrix products, arithmetic and copies ran while one was open for 0% -> 0% of each run, Pallas kernels for 0% -> 0%
where the time goes in v1:
time: 33.4 us; the launch traced here: 33.2 us
  Pallas kernels  29.7 us (89%)
  local copies, waits for them, and re-layouts  3.5 us (10%)
    pallas_call x1, Pallas kernels, body(): pl.pallas_call(functools.partial(kernel, n_row, n_col), out_shape=jax.Sha...  29.7 us
    unnamed x5, local copies, waits for them, and re-layouts  3.5 us

profile of v1, /device:TPU:0, one launch (start us, length us, event | category | flops | bytes accessed | tf_op | source)
XLA Modules:
  0.0 33.2 jit_solution(15899765799593300114)
XLA Ops:
  0.0 0.0 copy-start
  0.0 1.2 %copy-done = f32[2,256,512]{2,1,0:T(8,128)S(1)} copy-done((f32[2,256,512]{2,1,0:T(8,128)S(1)}, f32[2,256,512]{2,1,0:T(8,128)}, u32[]{:S(2)}) %copy-start) | copy-done | bytes 1048600
  1.2 0.0 copy-start.1
  1.2 0.9 %copy-done.1 = f32[2,512,64]{1,2,0:T(8,128)S(1)} copy-done((f32[2,512,64]{1,2,0:T(8,128)S(1)}, f32[2,512,64]{1,2,0:T(8,128)}, u32[]{:S(2)}) %copy-start.1) | copy-done | bytes 262168
  2.2 29.7 %shard_map.28 = f32[2,512,512]{2,1,0:T(8,128)S(1)} custom-call(f32[2,64,512]{2,1,0:T(8,128)S(1)} %bitcast.1, f32[2,256,512]{2,1,0:T(8,128)S(1)} %copy-done), custom_call_target="tpu_custom_call" | custom-call | tf_op jit(solution)/shard_map/pallas_call | solution.py:244
  31.9 1.3 %copy.4 = f32[2,512,512]{2,1,0:T(8,128)} copy(f32[2,512,512]{2,1,0:T(8,128)S(1)} %shard_map.28) | data formatting | bytes 4194304
Async XLA Ops:
  0.0 1.2 %copy-start = (f32[2,256,512]{2,1,0:T(8,128)S(1)}, f32[2,256,512]{2,1,0:T(8,128)}, u32[]{:S(2)}) copy-start(f32[2,256,512]{2,1,0:T(8,128)} %right_hbm.1) | copy-start | bytes 3145732
  1.2 0.9 %copy-start.1 = (f32[2,512,64]{1,2,0:T(8,128)S(1)}, f32[2,512,64]{1,2,0:T(8,128)}, u32[]{:S(2)}) copy-start(f32[2,512,64]{1,2,0:T(8,128)} %param.2) | copy-start | bytes 786436

commit v2 on v1

--- a/solution.py
+++ b/solution.py
@@ -20,10 +20,38 @@
     return jnp.dot(a, b, preferred_element_type=jnp.float32)
 
 
+def three_dots(left_hi, left_lo, w_hi, w_lo):
+    return dot(left_hi, w_hi) + (dot(left_hi, w_lo) + dot(left_lo, w_hi))
+
+
+def in_turn(kr):
+    return kr % LANES == 0
+
+
+def finish(first, done_ref, own_part, left_hi, left_lo, w_hi, w_lo, out_hbm, tail, sem):
+    rows, ready = done_ref.shape[1:]
+    early = pltpu.make_async_copy(done_ref, out_hbm.at[:, :, pl.ds(0, ready)], sem.at[0])
+    early.start()
+    copies = [early]
+    half = rows // 2
+    j = w_hi.shape[0] - 1
+    for i in range(2):
+        span = pl.ds(i * half, half)
+        total = own_part[span, :] + three_dots(
+            left_hi[span, first:], left_lo[span, first:], w_hi[j, first:, :], w_lo[j, first:, :])
+        tail[0, span, :] = total[:, :LANES]
+        tail[1, span, :] = total[:, LANES:]
+        copy = pltpu.make_async_copy(
+            tail.at[:, span, :], out_hbm.at[:, span, pl.ds(ready, LANES)], sem.at[1 + i])
+        copy.start()
+        copies.append(copy)
+    for copy in copies:
+        copy.wait()
+
+
 def kernel(
-    n_row, n_col, left_hbm, right_hbm, out_ref,
-    left_f32, right_f32, left_hi, left_lo, w_hi, w_lo,
-    own_sem, left_send, left_recv, right_send, right_recv,
+    n_row, n_col, left_hbm, right_hbm, out_ref, own_part, left_hi, left_lo, w_hi, w_lo,
+    left_f32, right_f32, own_sem, left_send, left_recv, right_send, right_recv,
 ):
     _, kb, rows = left_hbm.shape
     _, kr, cols = right_hbm.shape
@@ -115,14 +143,18 @@
     for part in range(2):
         across(z, part, True).start()
 
-    def to_weights(source_row, j, n):
-        span = pl.ds(pl.multiple_of(source_row, 8), n)
+    def to_weights(d, j):
+        owner = peer(d)
+        span = pl.ds(pl.multiple_of(owner * kr, 8), kr)
         re = split(right_f32[0, span, j * LANES:(j + 1) * LANES])
         im = split(right_f32[1, span, j * LANES:(j + 1) * LANES])
-        below = pl.ds(pl.multiple_of(depth + source_row, 8), n)
+        if in_turn(kr):
+            above, below = pl.ds(2 * d * kr, kr), pl.ds((2 * d + 1) * kr, kr)
+        else:
+            above, below = span, pl.ds(pl.multiple_of(depth + owner * kr, 8), kr)
         for w, a, b in ((w_hi, re[0], im[0]), (w_lo, re[1], im[1])):
-            w[j, span, :LANES] = a
-            w[j, span, LANES:] = b
+            w[j, above, :LANES] = a
+            w[j, above, LANES:] = b
             w[j, below, :LANES] = -b
             w[j, below, LANES:] = a
 
@@ -130,9 +162,23 @@
         for part in range(2):
             block = left_f32[part, pl.ds(pl.multiple_of(g * LANES, LANES), LANES), :].T
             high, low = split(block)
-            where = pl.ds(pl.multiple_of(part * depth + g * LANES, LANES), LANES)
+            if in_turn(kr):
+                owner = g * LANES // kr
+                turn = lax.rem(owner - x + n_row, n_row)
+                first = (2 * turn + part) * kr + g * LANES - owner * kr
+            else:
+                first = part * depth + g * LANES
+            where = pl.ds(pl.multiple_of(first, LANES), LANES)
             left_hi[:, where] = high
             left_lo[:, where] = low
+
+    def early_part():
+        if in_turn(kr):
+            n = 2 * kr
+            own_part[...] = three_dots(
+                left_hi[:, :n], left_lo[:, :n], w_hi[chunks - 1, :n, :], w_lo[chunks - 1, :n, :])
+        else:
+            own_part[...] = jnp.zeros_like(own_part)
 
     def partner_arrived(zz):
         for part in range(2):
@@ -146,11 +192,11 @@
     def right_arrived(j):
         for d in range(1, n_row):
             right_copy(d, j).wait_recv()
-            to_weights(lax.rem(x + n_row - d, n_row) * kr, j, kr)
+            to_weights(n_row - d, j)
 
     own_right.wait()
     for j in range(chunks):
-        to_weights(x * kr, j, kr)
+        to_weights(0, j)
     own_left.wait()
 
     for d in range(1, line):
@@ -204,12 +250,15 @@
         for g in range(depth // LANES):
             convert(g)
 
-    for j in range(chunks):
-        if j >= min(line - 1, chunks - 1):
+    for j in range(chunks - 1):
+        if j >= line - 1:
             right_arrived(j)
-        total = dot(left_hi[...], w_hi[j]) + (dot(left_hi[...], w_lo[j]) + dot(left_lo[...], w_hi[j]))
+        total = three_dots(left_hi[...], left_lo[...], w_hi[j], w_lo[j])
         out_ref[0, :, j * LANES:(j + 1) * LANES] = total[:, :LANES]
         out_ref[1, :, j * LANES:(j + 1) * LANES] = total[:, LANES:]
+        if j == chunks - 3 or (j == 0 and chunks < 3):
+            early_part()
+    right_arrived(chunks - 1)
 
     for j in range(chunks):
         for d in range(1, n_row):
@@ -241,18 +290,22 @@
     _, kb, rows = left.shape
     _, kr, cols = right_data.shape
     depth, chunks, line = kb * n_col, cols // LANES, n_col // 2
-    return pl.pallas_call(
+    vmem = pl.BlockSpec(memory_space=pltpu.VMEM)
+    held = pl.pallas_call(
         functools.partial(kernel, n_row, n_col),
-        out_shape=jax.ShapeDtypeStruct((2, rows, cols), jnp.float32),
-        in_specs=[pl.BlockSpec(memory_space=pl.ANY)] * 2,
-        out_specs=pl.BlockSpec(memory_space=pltpu.VMEM),
+        out_shape=[
+            jax.ShapeDtypeStruct((2, rows, cols - LANES), jnp.float32),
+            jax.ShapeDtypeStruct((rows, 2 * LANES), jnp.float32),
+            jax.ShapeDtypeStruct((rows, 2 * depth), jnp.bfloat16),
+            jax.ShapeDtypeStruct((rows, 2 * depth), jnp.bfloat16),
+            jax.ShapeDtypeStruct((chunks, 2 * depth, 2 * LANES), jnp.bfloat16),
+            jax.ShapeDtypeStruct((chunks, 2 * depth, 2 * LANES), jnp.bfloat16),
+        ],
+        in_specs=[pl.BlockSpec(memory_space=pltpu.HBM)] * 2,
+        out_specs=[vmem] * 6,
         scratch_shapes=[
             pltpu.VMEM((2, depth, rows), jnp.float32),
             pltpu.VMEM((2, depth, cols), jnp.float32),
-            pltpu.VMEM((rows, 2 * depth), jnp.bfloat16),
-            pltpu.VMEM((rows, 2 * depth), jnp.bfloat16),
-            pltpu.VMEM((chunks, 2 * depth, 2 * LANES), jnp.bfloat16),
-            pltpu.VMEM((chunks, 2 * depth, 2 * LANES), jnp.bfloat16),
             pltpu.SemaphoreType.DMA((2,)),
             pltpu.SemaphoreType.DMA((3, line, 2)),
             pltpu.SemaphoreType.DMA((2, line, 2)),
@@ -260,8 +313,16 @@
             pltpu.SemaphoreType.DMA((n_row - 1, chunks)),
         ],
         compiler_params=pltpu.CompilerParams(
-            collective_id=0, has_side_effects=True, vmem_limit_bytes=48 * 1024 * 1024),
+            collective_id=0, has_side_effects=True, vmem_limit_bytes=32 * 1024 * 1024),
     )(left, right_data)
+    return pl.pallas_call(
+        functools.partial(finish, 2 * kr if in_turn(kr) else 0),
+        out_shape=jax.ShapeDtypeStruct((2, rows, cols), jnp.float32),
+        in_specs=[vmem] * 6,
+        out_specs=pl.BlockSpec(memory_space=pltpu.HBM),
+        scratch_shapes=[pltpu.VMEM((2, rows, LANES), jnp.float32), pltpu.SemaphoreType.DMA((3,))],
+        compiler_params=pltpu.CompilerParams(vmem_limit_bytes=16 * 1024 * 1024),
+    )(*held)
 
 
 def solution(mesh):

time: 33.4 us -> 32.2 us (0.964)
  local copies, waits for them, and re-layouts: 3.5 us -> 2.17 us
    unnamed x5 -> x4, local copies, waits for them, and re-layouts: 3.5 us -> 2.17 us
    pallas_call x1 -> x2, Pallas kernels: 29.7 us -> 29.8 us  [the longest x1 28 us: body(): pl.pallas_call(functools.partial(kernel, n_row, n_col), out_shape=[jax.Sh...]
where the time goes in v2:
time: 32.2 us; the launch traced here: 32 us
  Pallas kernels  29.8 us (93%)
  local copies, waits for them, and re-layouts  2.17 us (7%)
    pallas_call x1, Pallas kernels, body(): pl.pallas_call(functools.partial(kernel, n_row, n_col), out_shape=[jax.Sh...  28 us
    unnamed x4, local copies, waits for them, and re-layouts  2.17 us
    pallas_call x1, Pallas kernels, body(): pl.pallas_call(functools.partial(finish, 2 * kr if in_turn(kr) else 0), o...  1.84 us

profile of v2, /device:TPU:0, one launch (start us, length us, event | category | flops | bytes accessed | tf_op | source)
XLA Modules:
  0.0 32.0 jit_solution(5966878771397657834)
XLA Ops:
  0.0 0.0 copy-start
  0.0 1.2 %copy-done = f32[2,256,512]{2,1,0:T(8,128)S(1)} copy-done((f32[2,256,512]{2,1,0:T(8,128)S(1)}, f32[2,256,512]{2,1,0:T(8,128)}, u32[]{:S(2)}) %copy-start) | copy-done | bytes 1048600
  1.2 0.0 copy-start.1
  1.2 0.9 %copy-done.1 = f32[2,512,64]{1,2,0:T(8,128)S(1)} copy-done((f32[2,512,64]{1,2,0:T(8,128)S(1)}, f32[2,512,64]{1,2,0:T(8,128)}, u32[]{:S(2)}) %copy-start.1) | copy-done | bytes 262168
  2.2 28.0 %shard_map.28 = (f32[2,512,384]{2,1,0:T(8,128)S(1)}, f32[512,256]{1,0:T(8,128)S(1)}, bf16[512,1024]{1,0:T(8,128)(2,1)S(1)}, bf16[512,1024]{1,0:T(8,128)(2,1)S(1)...) custom-call(f32[2,64,512]{2,1,0:T(8,128)S(1)} %bitcast.1, f32[2,256,512]{2,1,0:T(8,128)S(1)} %copy-done), custom_call_target="tpu_custom_call" | custom-call | tf_op jit(solution)/shard_map/pallas_call | solution.py:294
  30.2 1.8 %shard_map.29 = f32[2,512,512]{2,1,0:T(8,128)} custom-call(f32[2,512,384]{2,1,0:T(8,128)S(1)} %get-tuple-element.11.done_ref, f32[512,256]{1,0:T(8,128)S(1)} %get-tuple-element.12.own_part, bf16[512,1024]{1,0:T(8,128)(2,1)S(1)} %get-tuple-element.13.left_hi, bf16[512,1024]{1,0:T(8,128)(2,1)S(1)} %get-tuple-element.14.left_lo, ...), custom_call_target="tpu_custom_call" | custom-call | tf_op jit(solution)/shard_map/pallas_call | solution.py:318
Async XLA Ops:
  0.0 1.2 %copy-start = (f32[2,256,512]{2,1,0:T(8,128)S(1)}, f32[2,256,512]{2,1,0:T(8,128)}, u32[]{:S(2)}) copy-start(f32[2,256,512]{2,1,0:T(8,128)} %right_hbm.1) | copy-start | bytes 3145732
  1.2 0.9 %copy-start.1 = (f32[2,512,64]{1,2,0:T(8,128)S(1)}, f32[2,512,64]{1,2,0:T(8,128)}, u32[]{:S(2)}) copy-start(f32[2,512,64]{1,2,0:T(8,128)} %param.2) | copy-start | bytes 786436

commit v3 on v2

--- a/solution.py
+++ b/solution.py
@@ -314,7 +314,7 @@
         ],
         compiler_params=pltpu.CompilerParams(
             collective_id=0, has_side_effects=True, vmem_limit_bytes=32 * 1024 * 1024),
-    )(left, right_data)
+    )(pltpu.with_memory_space_constraint(left, pltpu.HBM), pltpu.with_memory_space_constraint(right_data, pltpu.HBM))
     return pl.pallas_call(
         functools.partial(finish, 2 * kr if in_turn(kr) else 0),
         out_shape=jax.ShapeDtypeStruct((2, rows, cols), jnp.float32),

time: 32.2 us -> 30.2 us (0.938)
  local copies, waits for them, and re-layouts: 2.17 us -> 0 us
    unnamed x4 -> x0, local copies, waits for them, and re-layouts: 2.17 us -> none
where the time goes in v3:
time: 30.2 us; the launch traced here: 30.1 us
  Pallas kernels  30 us (99%)
    pallas_call x1, Pallas kernels, body(): pl.pallas_call(functools.partial(kernel, n_row, n_col), out_shape=[jax.Sh...  28.2 us
    pallas_call x1, Pallas kernels, body(): pl.pallas_call(functools.partial(finish, 2 * kr if in_turn(kr) else 0), o...  1.84 us

profile of v3, /device:TPU:0, one launch (start us, length us, event | category | flops | bytes accessed | tf_op | source)
XLA Modules:
  0.0 30.1 jit_solution(4441440149178608989)
XLA Ops:
  0.0 28.2 %shard_map.28 = (f32[2,512,384]{2,1,0:T(8,128)S(1)}, f32[512,256]{1,0:T(8,128)S(1)}, bf16[512,1024]{1,0:T(8,128)(2,1)S(1)}, bf16[512,1024]{1,0:T(8,128)(2,1)S(1)...) custom-call(f32[2,64,512]{2,1,0:T(8,128)} %bitcast.1, f32[2,256,512]{2,1,0:T(8,128)} %right_hbm.1), custom_call_target="tpu_custom_call" | custom-call | tf_op jit(solution)/shard_map/pallas_call | solution.py:294
  28.2 1.8 %shard_map.29 = f32[2,512,512]{2,1,0:T(8,128)} custom-call(f32[2,512,384]{2,1,0:T(8,128)S(1)} %get-tuple-element.11.done_ref, f32[512,256]{1,0:T(8,128)S(1)} %get-tuple-element.12.own_part, bf16[512,1024]{1,0:T(8,128)(2,1)S(1)} %get-tuple-element.13.left_hi, bf16[512,1024]{1,0:T(8,128)(2,1)S(1)} %get-tuple-element.14.left_lo, ...), custom_call_target="tpu_custom_call" | custom-call | tf_op jit(solution)/shard_map/pallas_call | solution.py:318

commit v4 on v3

--- a/solution.py
+++ b/solution.py
@@ -26,6 +26,10 @@
 
 def in_turn(kr):
     return kr % LANES == 0
+
+
+def staged(n_row, kr, kb, line, chunks):
+    return n_row == 2 and in_turn(kr) and 2 * kb == LANES and line % 2 == 0 and chunks <= line
 
 
 def finish(first, done_ref, own_part, left_hi, left_lo, w_hi, w_lo, out_hbm, tail, sem):
@@ -172,13 +176,19 @@
             left_hi[:, where] = high
             left_lo[:, where] = low
 
-    def early_part():
-        if in_turn(kr):
-            n = 2 * kr
-            own_part[...] = three_dots(
-                left_hi[:, :n], left_lo[:, :n], w_hi[chunks - 1, :n, :], w_lo[chunks - 1, :n, :])
-        else:
-            own_part[...] = jnp.zeros_like(own_part)
+    early = staged(n_row, kr, kb, line, chunks)
+    near_own = z // max(line // 2, 1) == x
+
+    def piece(j, turn, fresh):
+        span = slice(turn * 2 * kr, (turn + 1) * 2 * kr)
+        total = three_dots(left_hi[:, span], left_lo[:, span], w_hi[j, span, :], w_lo[j, span, :])
+        if j == chunks - 1:
+            own_part[...] = total
+            return
+        where = slice(j * LANES, (j + 1) * LANES)
+        for part in range(2):
+            term = total[:, part * LANES:(part + 1) * LANES]
+            out_ref[part, :, where] = term if fresh else out_ref[part, :, where] + term
 
     def partner_arrived(zz):
         for part in range(2):
@@ -235,6 +245,19 @@
         if d - 1 < chunks - 1:
             right_arrived(d - 1)
 
+        if early and d >= line // 2:
+            first = d == line // 2
+
+            @pl.when(near_own)
+            def _():
+                for j in range(chunks) if first else ():
+                    piece(j, 0, True)
+
+            @pl.when(jnp.logical_not(near_own))
+            def _():
+                for j in range(0 if first else d - 1, min(d, chunks - 1)):
+                    piece(j, 1, True)
+
     if line == 1:
         settle(z)
     else:
@@ -250,14 +273,24 @@
         for g in range(depth // LANES):
             convert(g)
 
-    for j in range(chunks - 1):
-        if j >= line - 1:
-            right_arrived(j)
-        total = three_dots(left_hi[...], left_lo[...], w_hi[j], w_lo[j])
-        out_ref[0, :, j * LANES:(j + 1) * LANES] = total[:, :LANES]
-        out_ref[1, :, j * LANES:(j + 1) * LANES] = total[:, LANES:]
-        if j == chunks - 3 or (j == 0 and chunks < 3):
-            early_part()
+    if early:
+        @pl.when(near_own)
+        def _():
+            for j in range(chunks - 1):
+                piece(j, 1, False)
+
+        @pl.when(jnp.logical_not(near_own))
+        def _():
+            for j in range(chunks):
+                piece(j, 0, False)
+    else:
+        for j in range(chunks - 1):
+            if j >= line - 1:
+                right_arrived(j)
+            total = three_dots(left_hi[...], left_lo[...], w_hi[j], w_lo[j])
+            out_ref[0, :, j * LANES:(j + 1) * LANES] = total[:, :LANES]
+            out_ref[1, :, j * LANES:(j + 1) * LANES] = total[:, LANES:]
+        own_part[...] = jnp.zeros_like(own_part)
     right_arrived(chunks - 1)
 
     for j in range(chunks):
@@ -316,7 +349,7 @@
             collective_id=0, has_side_effects=True, vmem_limit_bytes=32 * 1024 * 1024),
     )(pltpu.with_memory_space_constraint(left, pltpu.HBM), pltpu.with_memory_space_constraint(right_data, pltpu.HBM))
     return pl.pallas_call(
-        functools.partial(finish, 2 * kr if in_turn(kr) else 0),
+        functools.partial(finish, 2 * kr if staged(n_row, kr, kb, line, chunks) else 0),
         out_shape=jax.ShapeDtypeStruct((2, rows, cols), jnp.float32),
         in_specs=[vmem] * 6,
         out_specs=pl.BlockSpec(memory_space=pltpu.HBM),

time: 30.2 us -> 30.2 us (level)
  no operation moved by 1% of the time
where the time goes in v4:
time: 30.2 us; the launch traced here: 30.1 us
  Pallas kernels  30 us (99%)
    pallas_call x1, Pallas kernels, body(): pl.pallas_call(functools.partial(kernel, n_row, n_col), out_shape=[jax.Sh...  28.2 us
    pallas_call x1, Pallas kernels, body(): pl.pallas_call(functools.partial(finish, 2 * kr if staged(n_row, kr, kb,...  1.84 us

profile of v4, /device:TPU:0, one launch (start us, length us, event | category | flops | bytes accessed | tf_op | source)
XLA Modules:
  0.0 30.1 jit_solution(12714558823630236489)
XLA Ops:
  0.0 28.2 %shard_map.28 = (f32[2,512,384]{2,1,0:T(8,128)S(1)}, f32[512,256]{1,0:T(8,128)S(1)}, bf16[512,1024]{1,0:T(8,128)(2,1)S(1)}, bf16[512,1024]{1,0:T(8,128)(2,1)S(1)...) custom-call(f32[2,64,512]{2,1,0:T(8,128)} %bitcast.1, f32[2,256,512]{2,1,0:T(8,128)} %right_hbm.1), custom_call_target="tpu_custom_call" | custom-call | tf_op jit(solution)/shard_map/pallas_call | solution.py:327
  28.2 1.8 %shard_map.29 = f32[2,512,512]{2,1,0:T(8,128)} custom-call(f32[2,512,384]{2,1,0:T(8,128)S(1)} %get-tuple-element.11.done_ref, f32[512,256]{1,0:T(8,128)S(1)} %get-tuple-element.12.own_part, bf16[512,1024]{1,0:T(8,128)(2,1)S(1)} %get-tuple-element.13.left_hi, bf16[512,1024]{1,0:T(8,128)(2,1)S(1)} %get-tuple-element.14.left_lo, ...), custom_call_target="tpu_custom_call" | custom-call | tf_op jit(solution)/shard_map/pallas_call | solution.py:351
